TPU v7x, 128 devices: a whole 4x4x4 slice. The times are simulated.
128 devices in a mesh: blk: 16 (over y, x), tp: 8 (over z, core).
Axes of the slice: x: 4, y: 4, z: 4, core: 2. Of those that a mesh axis runs over, the one named last changes fastest.
Arguments:
- hidden_in: bfloat16 [8192, 6144], P('blk', 'tp'), may hold values from -40 to 40
- ln_gain: float32 [6144], replicated, may hold values from 0.1 to 1.9
- w_qkv: bfloat16 [6144, 3, 3072], P(None, None, 'tp'), may hold values from -1 to 1
- w_out: bfloat16 [3072, 6144], P('tp'), may hold values from -0.625 to 0.625
- doc_lengths: int32 [64], replicated, may hold values from 0 to 4096, as said below
- segment_ids: int32 [8192], P('blk'), may hold values from 0 to 63, as said below
- pair_table: int32 [16, 16], replicated, may hold values from 0 to 1, as said below
- page_table: int32 [512], P('blk'), may hold values from 0 to 511, as said below
Outputs:
- attn_out: bfloat16 [8192, 6144], P('blk', 'tp')
- page_cache: bfloat16 [2, 512, 16, 3072], P(None, 'blk', None, 'tp')
Inputs may be any that keep to these rules, and one draw needn't show every extreme that they name: `doc_lengths`: the 64 documents in stream order; they sum to 8192, the empty ones stand just before the last slot, which holds the stream's last document, and the second document has exactly 4096 tokens. segment_ids[t] is the number of documents that end at or before token t; the last token belongs to slot 63. pair_table[i, j] is 1 exactly where a token of block j of 512 tokens and a token at or after it in block i lie in one document. `page_table`: the 32 entries of one block of tokens are that block's own page numbers, each once.
All inputs are finite; a program needn't handle non-finite values.
Results may differ from a plain program's by a relative error of at most 0.014.
Values may be sent and summed in bfloat16 or wider, within the bound.
A program may use at most 256 MiB of HBM per device.

v0:
```python
import jax
import jax.numpy as jnp
from jax import lax
from jax.sharding import PartitionSpec as P

HD = 96
ROT = 24
PAGE = 16
EPSILON = 1e-05


def layer_norm(whole, ln_gain):
    values32 = whole.astype(jnp.float32)
    row_mean = jnp.mean(values32, axis=-1, keepdims=True)
    centred = values32 - row_mean
    row_var = jnp.mean(centred * centred, axis=-1, keepdims=True)
    return (centred * lax.rsqrt(row_var + EPSILON) * ln_gain).astype(jnp.bfloat16)


def doc_positions(token_index, doc_lengths, segment_ids):
    starts = jnp.cumsum(doc_lengths) - doc_lengths
    slots = jnp.arange(doc_lengths.shape[0], dtype=jnp.int32)
    in_document = segment_ids[:, None] == slots[None, :]
    offsets = jnp.sum(jnp.where(in_document, starts[None, :], 0), axis=1)
    return token_index - offsets


def rotary(head_block, positions):
    half_rot = ROT // 2
    frequency = 10000.0 ** (-(2.0 * jnp.arange(half_rot, dtype=jnp.float32)) / ROT)
    angles = positions.astype(jnp.float32)[:, None] * frequency[None, :]
    cosine = jnp.cos(angles)[:, None, :]
    sine_part = jnp.sin(angles)[:, None, :]
    lower_half = head_block[..., :half_rot]
    upper_half = head_block[..., half_rot:ROT]
    return jnp.concatenate(
        [
            lower_half * cosine - upper_half * sine_part,
            upper_half * cosine + lower_half * sine_part,
            head_block[..., ROT:],
        ],
        axis=-1,
    )


def per_device(hidden_in, ln_gain, w_qkv, w_out, doc_lengths, segment_ids, pair_table, page_table):
    row_count = hidden_in.shape[0]
    whole = lax.all_gather(hidden_in, "tp", axis=1, tiled=True)
    normed = layer_norm(whole, ln_gain)
    width = whole.shape[1]
    col_count = w_qkv.shape[2]
    head_count = col_count // HD
    projected = jnp.dot(
        normed, w_qkv.reshape(width, 3 * col_count), preferred_element_type=jnp.float32
    ).reshape(row_count, 3, head_count, HD)
    block_index = lax.axis_index("blk")
    token_index = block_index * row_count + jnp.arange(row_count, dtype=jnp.int32)
    positions = doc_positions(token_index, doc_lengths, segment_ids)
    queries = rotary(projected[:, 0], positions).astype(jnp.bfloat16)
    key_rows = rotary(projected[:, 1], positions).astype(jnp.bfloat16)
    values = projected[:, 2].astype(jnp.bfloat16)
    table_row = lax.dynamic_index_in_dim(pair_table, block_index, 0, keepdims=False)
    block_ids = jnp.arange(pair_table.shape[1], dtype=jnp.int32)
    scale = HD ** (-0.5)
    start_state = (
        jnp.full((head_count, row_count), -1e30, jnp.float32),
        jnp.zeros((head_count, row_count), jnp.float32),
        jnp.zeros((head_count, row_count, HD), jnp.float32),
    )
    key_piece = lax.all_gather(key_rows, "blk", axis=0, tiled=True)
    value_piece = lax.all_gather(values, "blk", axis=0, tiled=True)
    segment_piece = lax.all_gather(segment_ids, "blk", axis=0, tiled=True)
    piece_rows = key_piece.shape[0]
    key_index = jnp.arange(piece_rows, dtype=jnp.int32)
    matches = (key_index // row_count)[:, None] == block_ids[None, :]
    live = jnp.sum(jnp.where(matches, table_row[None, :], 0), axis=1) > 0

    def compute(previous):
        maxima, totals, weighted = previous
        scores = (
            jnp.einsum("qhd,khd->hqk", queries, key_piece, preferred_element_type=jnp.float32)
            * scale
        )
        allowed = (
            live[None, :]
            & (segment_ids[:, None] == segment_piece[None, :])
            & (key_index[None, :] <= token_index[:, None])
        )
        scores = jnp.where(allowed[None], scores, -jnp.inf)
        newest = jnp.maximum(maxima, jnp.max(scores, axis=-1))
        weights = jnp.exp(scores - newest[..., None])
        totals = jnp.sum(weights, axis=-1)
        weighted = jnp.einsum(
            "hqk,khd->hqd",
            weights.astype(jnp.bfloat16),
            value_piece,
            preferred_element_type=jnp.float32,
        )
        return (newest, totals, weighted)

    final = lax.cond(jnp.any(live), compute, lambda previous: previous, start_state)
    mixed = (final[2] / final[1][..., None]).astype(jnp.bfloat16)
    heads_out = jnp.transpose(mixed, (1, 0, 2)).reshape(row_count, col_count)
    partial_term = jnp.dot(heads_out, w_out, preferred_element_type=jnp.float32)
    attn_out = lax.psum_scatter(
        partial_term.astype(jnp.bfloat16), "tp", scatter_dimension=1, tiled=True
    )
    page_count = row_count // PAGE
    local_pages = page_table - block_index * page_count
    stacked = jnp.stack(
        [key_rows.reshape(page_count, PAGE, col_count), values.reshape(page_count, PAGE, col_count)]
    )
    page_cache = jnp.zeros_like(stacked).at[:, local_pages].set(stacked)
    return (attn_out, page_cache)


def solution(mesh):
    placed = (P("blk", "tp"), P(), P(None, None, "tp"), P("tp", None), P(), P("blk"), P(), P("blk"))
    return jax.shard_map(
        per_device,
        mesh=mesh,
        in_specs=placed,
        out_specs=(P("blk", "tp"), P(None, "blk", None, "tp")),
        check_vma=False,
    )
```

profile of v0, /device:TPU:1, one launch (start us, length us, event | category | flops | bytes accessed | tf_op | source)
XLA Modules:
  0.0 351.7 jit_solution(17223538342270474863)
XLA Ops:
  7.2 0.7 all-gather.6.cloned.1.call-update
  8.0 18.8 %copy.23 = bf16[6144,3,384]{0,2,1:T(8,128)(2,1)} copy(bf16[6144,3,384]{2,0,1:T(8,128)(2,1)} %param.12) | data formatting | bytes 28311552 | tf_op args[2]
  27.4 26.9 %all-gather.6.cloned.1.call-done = bf16[512,6144]{1,0:T(8,128)(2,1)} async-done(((bf16[512,768]{1,0:T(8,128)(2,1)}), bf16[512,6144]{1,0:T(8,128)(2,1)}) %all-gather.6.cloned.1.call-update) | async-done | bytes 6291472 | tf_op jit(solution)/shard_map/all_gather | solution.py:48
  54.4 3.8 %convert_reduce_fusion = f32[512]{0:T(512)S(1)} fusion(bf16[512,6144]{1,0:T(8,128)(2,1)} %all-gather.6.cloned.1.call-done), kind=kLoop, calls=%fused_computation.14 | loop fusion | flops 6290944 | bytes 6293504 | tf_op jit(solution)/shard_map/reduce_sum | solution.py:14
  58.2 4.6 %fusion.10 = f32[512]{0:T(512)S(1)} fusion(bf16[512,6144]{1,0:T(8,128)(2,1)} %all-gather.6.cloned.1.call-done, f32[512]{0:T(512)S(1)} %broadcast_multiply_fusion), kind=kLoop, calls=%fused_computation.17 | loop fusion | flops 12582400 | bytes 6295552 | tf_op jit(solution)/shard_map/reduce_sum | solution.py:16
  62.8 11.8 %fusion.14 = f32[512,3,4,96]{0,3,2,1:T(8,128)S(1)} fusion(bf16[3,4,96,6144]{3,2,1,0:T(8,128)(2,1)} %bitcast.33, bf16[512,6144]{1,0:T(8,128)(2,1)S(1)} %copy-done.2, f32[6144]{0:T(1024)S(1)} %copy-done.8, f32[512]{0:T(512)S(1)} %add_rsqrt_fusion, f32[512]{0:T(512)S(1)} %broadcast_multiply_fusion), kind=kOutput, calls=%fused_computation.22 | convolution fusion | flops 7263485952 | bytes 22835200 | tf_op jit(solution)/shard_map/dot_general | solution.py:53
  74.9 0.8 maximum_convert_fusion
  75.8 0.8 slice.58
  76.9 0.6 fusion.22
  78.2 19.2 %all-gather.1 = s32[16,1,512]{2,1,0:T(1,128)S(1)} all-gather(s32[1,1,512]{2,1,0:T(1,128)S(1)} %bitcast.36), channel_id=1, replica_groups=mesh['blk'=16,'tp'=8] {'blk'}, dimensions={0}, use_global_device_ids=true | all-gather | bytes 34816 | tf_op jit(solution)/shard_map/all_gather | solution.py:72
  97.5 43.4 %all-gather.8.cloned.1.call-done = bf16[8192,4,96]{0,2,1:T(8,128)(2,1)} async-done(((bf16[512,4,96]{0,2,1:T(8,128)(2,1)}), bf16[8192,4,96]{0,2,1:T(8,128)(2,1)}) %all-gather.8.cloned.1.call-update) | async-done | bytes 6291472 | tf_op jit(solution)/shard_map/all_gather | solution.py:70
  140.9 68.3 %all-gather.10.cloned.1.call-done = bf16[8192,1,4,96]{0,3,2,1:T(8,128)(2,1)} async-done(((bf16[512,1,4,96]{0,3,2,1:T(8,128)(2,1)}), bf16[8192,1,4,96]{0,3,2,1:T(8,128)(2,1)}) %all-gather.10.cloned.1.call-update) | async-done | bytes 6291472 | tf_op jit(solution)/shard_map/all_gather | solution.py:71
  209.2 85.0 %conditional.1 = (f32[4,512]{1,0:T(4,128)S(1)}, f32[4,512,96]{1,2,0:T(8,128)S(1)}) conditional(s32[]{:T(128)} %convert_element_type.56, () %tuple.16, (pred[8192]{0:T(1024)(128)(4,1)S(1)}, s32[512]{0:T(512)S(1)}, s32[8192]{0:T(1024)S(1)}, s32[8192]{0:T(1024)S(1)}, s32[]{:T(128)}, /*index=5*/s32[512]{0:T(512)S(1)}, bf16[512,4,96]{0,2,1:T(8,128)(2,1)S(1)}, ...), branch_computations={%region_6.7_spmd, %region_7.10_spmd} | conditional | flops 6643776000 | bytes 231997456 | solution.py:101
  209.2 5.8 %compare_and_fusion = pred[512,8192]{1,0:T(8,128)(4,1)} fusion(s32[8192]{0:T(1024)S(1)} %get-tuple-element.23, s32[8192]{0:T(1024)S(1)} %get-tuple-element.22, s32[512]{0:T(512)S(1)} %broadcast_add_fusion, s32[512]{0:T(512)S(1)} %get-tuple-element.21, pred[8192]{0:T(1024)(128)(4,1)S(1)} %get-tuple-element.20), kind=kLoop, calls=%fused_computation.8 | loop fusion | flops 16777216 | bytes 4272128 | tf_op jit(solution)/shard_map/cond/branch_1_fun/and | solution.py:85
  215.0 28.2 %fusion = (f32[4,512]{1,0:T(4,128)S(1)}, f32[4,512,8192]{2,1,0:T(8,128)}) fusion(pred[512,8192]{1,0:T(8,128)(4,1)} %compare_and_fusion, bf16[512,4,96]{0,2,1:T(8,128)(2,1)S(1)} %get-tuple-element.26, bf16[8192,4,96]{0,2,1:T(8,128)(2,1)} %get-tuple-element.27), kind=kOutput, calls=%fused_computation.3 | convolution fusion | flops 3271555072 | bytes 77996032 | tf_op jit(solution)/shard_map/cond/branch_1_fun/qhd,khd->hqk/dot_general | solution.py:81
  243.2 28.1 %fusion.3 = f32[4,512,96]{1,2,0:T(8,128)S(1)} fusion(bf16[8192,4,96]{0,2,1:T(8,128)(2,1)} %get-tuple-element.28, f32[4,512,8192]{2,1,0:T(8,128)} %get-tuple-element.38, f32[4,512]{1,0:T(4,128)S(1)} %broadcast_maximum_fusion, pred[512,8192]{1,0:T(8,128)(4,1)} %compare_and_fusion), kind=kOutput, calls=%fused_computation.6 | convolution fusion | flops 3288334336 | bytes 78389248 | tf_op jit(solution)/shard_map/cond/branch_1_fun/hqk,khd->hqd/dot_general | solution.py:93
  271.3 22.7 %fusion.2 = f32[4,512]{1,0:T(4,128)S(1)} fusion(f32[4,512,8192]{2,1,0:T(8,128)} %get-tuple-element.38, f32[4,512]{1,0:T(4,128)S(1)} %broadcast_maximum_fusion, pred[512,8192]{1,0:T(8,128)(4,1)} %compare_and_fusion), kind=kLoop, calls=%fused_computation.5 | loop fusion | flops 67106816 | bytes 71319552 | tf_op jit(solution)/shard_map/cond/branch_1_fun/reduce_sum | solution.py:92
  294.4 7.8 %convolution_convert_fusion = bf16[512,6144]{1,0:T(8,128)(2,1)} fusion(bf16[512,384]{0,1:T(8,128)(2,1)S(1)} %bitcast.34, bf16[384,6144]{1,0:T(8,128)(2,1)} %param.13), kind=kOutput, calls=%fused_computation.20 | convolution fusion | flops 2419064832 | bytes 11403264 | tf_op jit(solution)/shard_map/dot_general | solution.py:104
  302.2 0.3 copy.25
  302.6 0.3 copy.26
  302.9 0.4 convert_element_type.65
  303.3 0.4 convert_element_type.66
  303.9 2.3 scatter_fusion
  306.2 38.9 %reduce-scatter.2.cloned.1.call-done = bf16[512,768]{1,0:T(8,128)(2,1)} async-done(((bf16[512,6144]{1,0:T(8,128)(2,1)}), bf16[512,768]{1,0:T(8,128)(2,1)}) %reduce-scatter.2.cloned.1.call-update) | async-done | bytes 786448 | tf_op jit(solution)/shard_map/reduce_scatter | solution.py:105
  (55 shorter events, 1.8 us)
Async XLA Ops:
  7.2 69.5 %copy-start = (s32[16,16]{1,0:T(8,128)S(1)}, s32[16,16]{1,0:T(8,128)}, u32[]{:S(2)}) copy-start(s32[16,16]{1,0:T(8,128)} %param.16) | copy-start | bytes 3076
  7.2 47.2 %all-gather.6.cloned.1.call-start = ((), (), s32[]{:S(2)}) async-start(), calls=%async_computation.1 | async-start | bytes 7077888 | tf_op jit(solution)/shard_map/all_gather | solution.py:48
  7.9 133.0 %all-gather.8.cloned.1.call-start = ((), (), s32[]{:S(2)}) async-start(), calls=%async_computation.2 | async-start | bytes 6684672 | tf_op jit(solution)/shard_map/all_gather | solution.py:70
  8.0 18.8 %copy-start.7 = (s32[64]{0:T(128)S(1)}, s32[64]{0:T(128)}, u32[]{:S(2)}) copy-start(s32[64]{0:T(128)} %param.14) | copy-start | bytes 772
  8.0 19.2 %copy-start.6 = (s32[512]{0:T(512)S(1)}, s32[512]{0:T(512)}, u32[]{:S(2)}) copy-start(s32[512]{0:T(512)} %param.15) | copy-start | bytes 6148
  26.8 36.0 %copy-start.8 = (f32[6144]{0:T(1024)S(1)}, f32[6144]{0:T(1024)}, u32[]{:S(2)}) copy-start(f32[6144]{0:T(1024)} %param.11) | copy-start | bytes 73732
  54.4 8.4 %copy-start.2 = (bf16[512,6144]{1,0:T(8,128)(2,1)S(1)}, bf16[512,6144]{1,0:T(8,128)(2,1)}, u32[]{:S(2)}) copy-start(bf16[512,6144]{1,0:T(8,128)(2,1)} %all-gather.6.cloned.1.call-done) | copy-start | bytes 18874372
  75.7 133.5 %all-gather.10.cloned.1.call-start = ((), (), s32[]{:S(2)}) async-start(), calls=%async_computation.4 | async-start | bytes 6684672 | tf_op jit(solution)/shard_map/all_gather | solution.py:71
  76.6 268.6 %reduce-scatter.2.cloned.1.call-start = ((), (), s32[]{:S(2)}) async-start(), calls=%async_computation.3 | async-start | bytes 7077888 | tf_op jit(solution)/shard_map/reduce_scatter | solution.py:105
  294.2 8.0 %copy-start.9 = (s32[32]{0:T(128)S(1)}, s32[32]{0:T(128)}, u32[]{:S(2)}) copy-start(s32[32]{0:T(128)} %param.17) | copy-start | bytes 388
  294.2 8.0 %copy-start.3 = (bf16[512,4,96]{0,2,1:T(8,128)(2,1)S(1)}, bf16[512,4,96]{0,2,1:T(8,128)(2,1)}, u32[]{:S(2)}) copy-start(bf16[512,4,96]{0,2,1:T(8,128)(2,1)} %maximum_convert_fusion) | copy-start | bytes 1179652
  294.3 8.3 %copy-start.4 = (bf16[512,1,4,96]{0,3,2,1:T(8,128)(2,1)S(1)}, bf16[512,1,4,96]{0,3,2,1:T(8,128)(2,1)}, u32[]{:S(2)}) copy-start(bf16[512,1,4,96]{0,3,2,1:T(8,128)(2,1)} %slice.58) | copy-start | bytes 1179652
  294.4 50.8 %copy-start.1 = (s32[16,16]{1,0:T(8,128)S(1)}, s32[16,16]{1,0:T(8,128)}, u32[]{:S(2)}) copy-start(s32[16,16]{1,0:T(8,128)} %param.16) | copy-start | bytes 3076
  306.2 38.9 %copy-start.5 = (bf16[2,32,16,384]{3,2,1,0:T(8,128)(2,1)}, bf16[2,32,16,384]{3,2,1,0:T(8,128)(2,1)S(1)}, u32[]{:S(2)}) copy-start(bf16[2,32,16,384]{3,2,1,0:T(8,128)(2,1)S(1)} %scatter_fusion) | copy-start | bytes 2359300
Sparse Core Ops, SparseCore 0:
  9.7 44.6 all-gather.5
  75.8 64.9 all-gather.7
  143.0 66.1 all-gather.9
  302.3 42.7 reduce-scatter.1
where the time goes:
time: 352 us
  waiting for transfers between devices  178 us (51%)
  matrix products  75.9 us (22%)
  other arithmetic  39.4 us (11%)
  local copies, waits for them, and re-layouts  23.8 us (7%)
  blocking collectives  19.2 us (5%)
  between operations  14.7 us (4%)
    all_gather x1, waiting for transfers between devices, per_device(): value_piece = lax.all_gather(values, 'blk', axis=0, tiled=True)  68.3 us
    all_gather x1, waiting for transfers between devices, per_device(): key_piece = lax.all_gather(key_rows, 'blk', axis=0, tiled=True)  43.4 us
    reduce_scatter x1, waiting for transfers between devices, per_device(): lax.psum_scatter(partial_term.astype(jnp.bfloat16), 'tp', scatter_dimensi...  38.9 us
    dot_general x1, matrix products, compute(): jnp.einsum('qhd,khd->hqk', queries, key_piece, preferred_element_type=jnp...  28.2 us
    dot_general x1, matrix products, compute(): jnp.einsum('hqk,khd->hqd', weights.astype(jnp.bfloat16), value_piece, pre...  28.1 us
    all_gather x1, waiting for transfers between devices, per_device(): whole = lax.all_gather(hidden_in, 'tp', axis=1, tiled=True)  26.9 us
    reduce_sum x1, other arithmetic, compute(): totals = jnp.sum(weights, axis=-1)  22.7 us
    all_gather x1, blocking collectives, per_device(): segment_piece = lax.all_gather(segment_ids, 'blk', axis=0, tiled=True)  19.2 us
  transfers between devices with their start and end apart: 4, of which 4 were waited for; matrix products, arithmetic and copies ran while one was open for 7% of the time, Pallas kernels for 0%

commit v1 on v0

--- a/solution.py
+++ b/solution.py
@@ -45,7 +45,8 @@
 
 def per_device(hidden_in, ln_gain, w_qkv, w_out, doc_lengths, segment_ids, pair_table, page_table):
     row_count = hidden_in.shape[0]
-    whole = lax.all_gather(hidden_in, "tp", axis=1, tiled=True)
+    sent = jnp.stack([hidden_in] * lax.axis_size("tp"))
+    whole = jnp.concatenate(lax.all_to_all(sent, "tp", 0, 0), axis=1)
     normed = layer_norm(whole, ln_gain)
     width = whole.shape[1]
     col_count = w_qkv.shape[2]

time: 352 us -> 397 us (1.13)
  waiting for transfers between devices: 178 us -> 203 us
  local copies, waits for them, and re-layouts: 23.8 us -> 36.5 us
  starting transfers between devices: 0.16 us -> 6.89 us
    all_to_all x0 -> x1, waiting for transfers between devices: none -> 51.9 us  [per_device(): whole = jnp.concatenate(lax.all_to_all(sent, 'tp', 0, 0), axis=1)]
    all_gather x1 -> x0, waiting for transfers between devices: 26.9 us -> none  [per_device(): whole = lax.all_gather(hidden_in, 'tp', axis=1, tiled=True)]
    all_to_all x0 -> x1, local copies, waits for them, and re-layouts: none -> 8.65 us  [per_device(): whole = jnp.concatenate(lax.all_to_all(sent, 'tp', 0, 0), axis=1)]
    all_to_all x0 -> x1, starting transfers between devices: none -> 6.8 us  [per_device(): whole = jnp.concatenate(lax.all_to_all(sent, 'tp', 0, 0), axis=1)]
    another operation x1 -> x2, local copies, waits for them, and re-layouts: 0.1 us -> 4.3 us  [the longest x1 4.2 us: per_device(): sent = jnp.stack([hidden_in] * lax.axis_size('tp'))]
  transfers between devices with their start and end apart: 4 -> 4, of which waited for: 4 -> 4; matrix products, arithmetic and copies ran while one was open for 7% -> 6% of each run, Pallas kernels for 0% -> 0%
where the time goes in v1:
time: 397 us; the launch traced here: 396 us
  waiting for transfers between devices  203 us (51%)
  matrix products  74.3 us (19%)
  other arithmetic  41.3 us (10%)
  local copies, waits for them, and re-layouts  36.5 us (9%)
  blocking collectives  19.5 us (5%)
  between operations  14.7 us (4%)
  starting transfers between devices  6.89 us (2%)
    all_gather x1, waiting for transfers between devices, per_device(): value_piece = lax.all_gather(values, 'blk', axis=0, tiled=True)  68.3 us
    all_to_all x1, waiting for transfers between devices, per_device(): whole = jnp.concatenate(lax.all_to_all(sent, 'tp', 0, 0), axis=1)  51.9 us
    all_gather x1, waiting for transfers between devices, per_device(): key_piece = lax.all_gather(key_rows, 'blk', axis=0, tiled=True)  43.4 us
    reduce_scatter x1, waiting for transfers between devices, per_device(): lax.psum_scatter(partial_term.astype(jnp.bfloat16), 'tp', scatter_dimensi...  38.9 us
    dot_general x1, matrix products, compute(): jnp.einsum('qhd,khd->hqk', queries, key_piece, preferred_element_type=jnp...  28.2 us
    dot_general x1, matrix products, compute(): jnp.einsum('hqk,khd->hqd', weights.astype(jnp.bfloat16), value_piece, pre...  28.1 us
    reduce_sum x1, other arithmetic, compute(): totals = jnp.sum(weights, axis=-1)  22.7 us
    all_gather x1, blocking collectives, per_device(): segment_piece = lax.all_gather(segment_ids, 'blk', axis=0, tiled=True)  19.5 us
  transfers between devices with their start and end apart: 4, of which 4 were waited for; matrix products, arithmetic and copies ran while one was open for 6% of the time, Pallas kernels for 0%

profile of v1, /device:TPU:1, one launch (start us, length us, event | category | flops | bytes accessed | tf_op | source)
XLA Modules:
  0.0 396.0 jit_solution(484392015133474613)
XLA Ops:
  7.2 4.2 %stack.4 = bf16[8,512,768]{2,1,0:T(8,128)(2,1)} broadcast(bf16[512,768]{1,0:T(8,128)(2,1)} %param.10), dimensions={1,2} | broadcast | bytes 7077888 | tf_op jit(solution)/shard_map/stack | solution.py:48
  11.4 6.8 %all-to-all-start = ((bf16[8,512,768]{2,1,0:T(8,128)(2,1)}), bf16[8,512,768]{2,1,0:T(8,128)(2,1)}, u32[]{:S(2)}, u32[]{:S(2)}) async-start(bf16[8,512,768]{2,1,0:T(8,128)(2,1)} %stack.4), calls=%async_computation | async-start | bytes 12582912 | tf_op jit(solution)/shard_map/all_to_all | solution.py:49
  18.2 18.6 %copy.31 = bf16[6144,3,384]{0,2,1:T(8,128)(2,1)} copy(bf16[6144,3,384]{2,0,1:T(8,128)(2,1)} %param.12) | data formatting | bytes 28311552 | tf_op args[2]
  37.5 51.9 %all-to-all-done = bf16[8,512,768]{2,1,0:T(8,128)(2,1)} async-done(((bf16[8,512,768]{2,1,0:T(8,128)(2,1)}), bf16[8,512,768]{2,1,0:T(8,128)(2,1)}, u32[]{:S(2)}, u32[]{:S(2)}) %all-to-all-start) | async-done | bytes 6291488 | tf_op jit(solution)/shard_map/all_to_all | solution.py:49
  89.4 8.7 %copy.30 = bf16[8,512,768]{1,2,0:T(8,128)(2,1)} copy(bf16[8,512,768]{2,1,0:T(8,128)(2,1)} %all-to-all-done) | data formatting | bytes 12582912 | tf_op jit(solution)/shard_map/all_to_all | solution.py:49
  98.1 3.8 convert_reduce_fusion
  101.9 4.5 %fusion.10 = f32[512]{0:T(512)S(1)} fusion(bf16[8,512,768]{1,2,0:T(8,128)(2,1)} %copy.30, f32[512]{0:T(512)S(1)} %broadcast_multiply_fusion), kind=kLoop, calls=%fused_computation.17 | loop fusion | flops 12582400 | bytes 6295552 | tf_op jit(solution)/shard_map/reduce_sum | solution.py:16
  106.4 2.0 fusion.12
  108.4 10.3 %fusion.17 = f32[512,3,4,96]{0,3,2,1:T(8,128)S(1)} fusion(bf16[512,6144,1,1]{0,1,3,2:T(8,128)(2,1)S(1)} %bitcast.35, bf16[3,4,96,6144]{3,2,1,0:T(8,128)(2,1)} %bitcast.34), kind=kOutput, calls=%fused_computation.54 | convolution fusion | flops 7247757312 | bytes 22806528 | tf_op jit(solution)/shard_map/dot_general | solution.py:54
  118.9 0.8 maximum_convert_fusion
  119.8 0.8 slice.58
  120.9 0.6 fusion.16
  122.2 19.5 %all-gather.1 = s32[16,1,512]{2,1,0:T(1,128)S(1)} all-gather(s32[1,1,512]{2,1,0:T(1,128)S(1)} %bitcast.38), channel_id=1, replica_groups=mesh['blk'=16,'tp'=8] {'blk'}, dimensions={0}, use_global_device_ids=true | all-gather | bytes 34816 | tf_op jit(solution)/shard_map/all_gather | solution.py:73
  141.8 43.4 %all-gather.5.cloned.1.call-done = bf16[8192,4,96]{0,2,1:T(8,128)(2,1)} async-done(((bf16[512,4,96]{0,2,1:T(8,128)(2,1)}), bf16[8192,4,96]{0,2,1:T(8,128)(2,1)}) %all-gather.5.cloned.1.call-update) | async-done | bytes 6291472 | tf_op jit(solution)/shard_map/all_gather | solution.py:71
  185.2 68.3 %all-gather.7.cloned.1.call-done = bf16[8192,1,4,96]{0,3,2,1:T(8,128)(2,1)} async-done(((bf16[512,1,4,96]{0,3,2,1:T(8,128)(2,1)}), bf16[8192,1,4,96]{0,3,2,1:T(8,128)(2,1)}) %all-gather.7.cloned.1.call-update) | async-done | bytes 6291472 | tf_op jit(solution)/shard_map/all_gather | solution.py:72
  253.5 85.0 %conditional.1 = (f32[4,512]{1,0:T(4,128)S(1)}, f32[4,512,96]{1,2,0:T(8,128)S(1)}) conditional(s32[]{:T(128)} %convert_element_type.61, () %tuple.16, (pred[8192]{0:T(1024)(128)(4,1)S(1)}, s32[512]{0:T(512)S(1)}, s32[8192]{0:T(1024)S(1)}, s32[8192]{0:T(1024)S(1)}, s32[]{:T(128)}, /*index=5*/s32[512]{0:T(512)S(1)}, bf16[512,4,96]{0,2,1:T(8,128)(2,1)S(1)}, ...), branch_computations={%region_6.7_spmd, %region_7.10_spmd} | conditional | flops 6643776000 | bytes 231997456 | solution.py:102
  253.5 5.8 %compare_and_fusion = pred[512,8192]{1,0:T(8,128)(4,1)} fusion(s32[8192]{0:T(1024)S(1)} %get-tuple-element.23, s32[8192]{0:T(1024)S(1)} %get-tuple-element.22, s32[512]{0:T(512)S(1)} %broadcast_add_fusion, s32[512]{0:T(512)S(1)} %get-tuple-element.21, pred[8192]{0:T(1024)(128)(4,1)S(1)} %get-tuple-element.20), kind=kLoop, calls=%fused_computation.8 | loop fusion | flops 16777216 | bytes 4272128 | tf_op jit(solution)/shard_map/cond/branch_1_fun/and | solution.py:86
  259.3 28.2 %fusion = (f32[4,512]{1,0:T(4,128)S(1)}, f32[4,512,8192]{2,1,0:T(8,128)}) fusion(pred[512,8192]{1,0:T(8,128)(4,1)} %compare_and_fusion, bf16[512,4,96]{0,2,1:T(8,128)(2,1)S(1)} %get-tuple-element.26, bf16[8192,4,96]{0,2,1:T(8,128)(2,1)} %get-tuple-element.27), kind=kOutput, calls=%fused_computation.3 | convolution fusion | flops 3271555072 | bytes 77996032 | tf_op jit(solution)/shard_map/cond/branch_1_fun/qhd,khd->hqk/dot_general | solution.py:82
  287.5 28.1 %fusion.3 = f32[4,512,96]{1,2,0:T(8,128)S(1)} fusion(bf16[8192,4,96]{0,2,1:T(8,128)(2,1)} %get-tuple-element.28, f32[4,512,8192]{2,1,0:T(8,128)} %get-tuple-element.38, f32[4,512]{1,0:T(4,128)S(1)} %broadcast_maximum_fusion, pred[512,8192]{1,0:T(8,128)(4,1)} %compare_and_fusion), kind=kOutput, calls=%fused_computation.6 | convolution fusion | flops 3288334336 | bytes 78389248 | tf_op jit(solution)/shard_map/cond/branch_1_fun/hqk,khd->hqd/dot_general | solution.py:94
  315.6 22.7 %fusion.2 = f32[4,512]{1,0:T(4,128)S(1)} fusion(f32[4,512,8192]{2,1,0:T(8,128)} %get-tuple-element.38, f32[4,512]{1,0:T(4,128)S(1)} %broadcast_maximum_fusion, pred[512,8192]{1,0:T(8,128)(4,1)} %compare_and_fusion), kind=kLoop, calls=%fused_computation.5 | loop fusion | flops 67106816 | bytes 71319552 | tf_op jit(solution)/shard_map/cond/branch_1_fun/reduce_sum | solution.py:93
  338.7 7.8 %convolution_convert_fusion = bf16[512,6144]{1,0:T(8,128)(2,1)} fusion(bf16[512,384]{0,1:T(8,128)(2,1)S(1)} %bitcast.36, bf16[384,6144]{1,0:T(8,128)(2,1)} %param.13), kind=kOutput, calls=%fused_computation.20 | convolution fusion | flops 2419064832 | bytes 11403264 | tf_op jit(solution)/shard_map/dot_general | solution.py:105
  347.5 0.4 convert_element_type.71
  348.2 2.3 scatter_fusion
  350.5 38.9 %reduce-scatter.2.cloned.1.call-done = bf16[512,768]{1,0:T(8,128)(2,1)} async-done(((bf16[512,6144]{1,0:T(8,128)(2,1)}), bf16[512,768]{1,0:T(8,128)(2,1)}) %reduce-scatter.2.cloned.1.call-update) | async-done | bytes 786448 | tf_op jit(solution)/shard_map/reduce_scatter | solution.py:106
  (58 shorter events, 2.7 us)
Async XLA Ops:
  7.2 113.5 %copy-start = (s32[16,16]{1,0:T(8,128)S(1)}, s32[16,16]{1,0:T(8,128)}, u32[]{:S(2)}) copy-start(s32[16,16]{1,0:T(8,128)} %param.16) | copy-start | bytes 3076
  7.2 11.0 %copy-start.6 = (f32[6144]{0:T(1024)S(1)}, f32[6144]{0:T(1024)}, u32[]{:S(2)}) copy-start(f32[6144]{0:T(1024)} %param.11) | copy-start | bytes 73732
  11.4 78.1 %all-to-all-start = ((bf16[8,512,768]{2,1,0:T(8,128)(2,1)}), bf16[8,512,768]{2,1,0:T(8,128)(2,1)}, u32[]{:S(2)}, u32[]{:S(2)}) async-start(bf16[8,512,768]{2,1,0:T(8,128)(2,1)} %stack.4), calls=%async_computation | async-start | bytes 12582912 | tf_op jit(solution)/shard_map/all_to_all | solution.py:49
  18.2 167.0 %all-gather.5.cloned.1.call-start = ((), (), s32[]{:S(2)}) async-start(), calls=%async_computation.2 | async-start | bytes 6684672 | tf_op jit(solution)/shard_map/all_gather | solution.py:71
  18.2 18.6 %copy-start.8 = (s32[64]{0:T(128)S(1)}, s32[64]{0:T(128)}, u32[]{:S(2)}) copy-start(s32[64]{0:T(128)} %param.14) | copy-start | bytes 772
  18.2 19.0 %copy-start.7 = (s32[512]{0:T(512)S(1)}, s32[512]{0:T(512)}, u32[]{:S(2)}) copy-start(s32[512]{0:T(512)} %param.15) | copy-start | bytes 6148
  98.1 8.3 %copy-start.2 = (bf16[8,512,768]{1,2,0:T(8,128)(2,1)S(1)}, bf16[8,512,768]{1,2,0:T(8,128)(2,1)}, u32[]{:S(2)}) copy-start(bf16[8,512,768]{1,2,0:T(8,128)(2,1)} %copy.30) | copy-start | bytes 18874372
  119.8 133.7 %all-gather.7.cloned.1.call-start = ((), (), s32[]{:S(2)}) async-start(), calls=%async_computation.4 | async-start | bytes 6684672 | tf_op jit(solution)/shard_map/all_gather | solution.py:72
  120.6 268.8 %reduce-scatter.2.cloned.1.call-start = ((), (), s32[]{:S(2)}) async-start(), calls=%async_computation.3 | async-start | bytes 7077888 | tf_op jit(solution)/shard_map/reduce_scatter | solution.py:106
  338.5 8.0 %copy-start.9 = (s32[32]{0:T(128)S(1)}, s32[32]{0:T(128)}, u32[]{:S(2)}) copy-start(s32[32]{0:T(128)} %param.17) | copy-start | bytes 388
  338.5 8.0 %copy-start.3 = (bf16[512,4,96]{0,2,1:T(8,128)(2,1)S(1)}, bf16[512,4,96]{0,2,1:T(8,128)(2,1)}, u32[]{:S(2)}) copy-start(bf16[512,4,96]{0,2,1:T(8,128)(2,1)} %maximum_convert_fusion) | copy-start | bytes 1179652
  338.5 8.3 %copy-start.4 = (bf16[512,1,4,96]{0,3,2,1:T(8,128)(2,1)S(1)}, bf16[512,1,4,96]{0,3,2,1:T(8,128)(2,1)}, u32[]{:S(2)}) copy-start(bf16[512,1,4,96]{0,3,2,1:T(8,128)(2,1)} %slice.58) | copy-start | bytes 1179652
  338.6 50.8 %copy-start.1 = (s32[16,16]{1,0:T(8,128)S(1)}, s32[16,16]{1,0:T(8,128)}, u32[]{:S(2)}) copy-start(s32[16,16]{1,0:T(8,128)} %param.16) | copy-start | bytes 3076
  350.5 38.9 %copy-start.5 = (bf16[2,32,16,384]{3,2,1,0:T(8,128)(2,1)}, bf16[2,32,16,384]{3,2,1,0:T(8,128)(2,1)S(1)}, u32[]{:S(2)}) copy-start(bf16[2,32,16,384]{3,2,1,0:T(8,128)(2,1)S(1)} %scatter_fusion) | copy-start | bytes 2359300
Sparse Core Ops, SparseCore 0:
  119.9 65.2 all-gather.4
  187.3 66.1 all-gather.6
  346.6 42.7 reduce-scatter.1
